TPU v7x, 32 devices: a whole 2x2x4 slice. The times are simulated.
32 devices in a mesh: slab: 8 (over y, x, core), pencil: 4 (over z).
Axes of the slice: x: 2, y: 2, z: 4, core: 2. Of those that a mesh axis runs over, the one named last changes fastest.
Arguments:
- template: float32 [256, 256, 256], P('slab', 'pencil'), may hold values from -6 to 6
- fixed_image: float32 [256, 256, 256], P('slab', 'pencil'), may hold values from -6 to 6
- velocity: float32 [3, 256, 256, 256], P(None, 'slab', 'pencil'), may hold values from -2 to 2
- src_owner: int32 [512, 2], P(('slab', 'pencil')), may hold values from 0 to 7, all different within a row; in each aligned block of 16 rows (0 to 15, 16 to 31, ...) at most 4 rows name the same one
- src_local: int32 [512, 2], P(('slab', 'pencil')), may hold values from 0 to 15
- weights: float32 [512, 2], P(('slab', 'pencil')), may hold values from 0.2 to 1
Outputs:
- gradient: float32 [3, 256, 256, 256], P(None, 'slab', 'pencil')
Inputs may be any that keep to these rules, and one draw needn't show every extreme that they name: `src_owner`: within the 16 rows of one device no owner is named more than 4 times, a bound that some block reaches; each row names 2 different owners.
All inputs are finite; a program needn't handle non-finite values.
Results may differ from a plain program's by a relative error of at most 0.00007.
Values sent between devices are 32-bit elements; how exact they have to be, the bound alone decides.
A program may use at most 192 MiB of HBM per device.

v0:
```python
import functools

import jax
import jax.numpy as jnp
from jax import lax
from jax.experimental import pallas as pl
from jax.experimental.pallas import tpu as pltpu
from jax.sharding import PartitionSpec as P

EDGE = 32
LANES = 128
QUADS = LANES // EDGE
MESH = pl.DeviceIdType.MESH
LIMIT = 50 * 1024 * 1024

smooth_weight = 0.1
time_step = 0.5


def whole(memory_space=pltpu.VMEM):
    return pl.BlockSpec(memory_space=memory_space)


def params(**kw):
    return pltpu.CompilerParams(vmem_limit_bytes=LIMIT, **kw)


def slots_kernel(owner_ref, local_ref, weight_ref, ids_ref, brick_ref, slot_weight_ref, count_ref):
    readers, capacity = ids_ref.shape
    bricks, picks = owner_ref.shape

    def clear(i, carry):
        count_ref[i] = 0
        for c in range(capacity):
            ids_ref[i, c] = 0
            brick_ref[i, c] = 0
            slot_weight_ref[i, c] = 0.0
        return carry

    lax.fori_loop(0, readers, clear, 0)

    def place(g, carry):
        for k in range(picks):
            owner = owner_ref[g, k]
            slot = count_ref[owner]
            count_ref[owner] = slot + 1
            ids_ref[owner, slot] = local_ref[g, k]
            brick_ref[owner, slot] = g
            slot_weight_ref[owner, slot] = weight_ref[g, k]
        return carry

    lax.fori_loop(0, bricks, place, 0)


def masks_of(brick_ref, weight_ref, lead, sign, part, tile_count):
    capacity = brick_ref.shape[1]
    quad = lax.broadcasted_iota(jnp.int32, (8, LANES), 1) // EDGE
    masks = [[] for _ in range(tile_count)]
    for r in range(QUADS):
        brick = jnp.full((8, LANES), -1, jnp.int32)
        weight = jnp.ones((8, LANES), jnp.float32)
        for j in range(QUADS):
            q = (j - sign * r) % QUADS
            if q // capacity == part:
                brick = jnp.where(quad == j, brick_ref[lead, q % capacity], brick)
                if weight_ref is not None:
                    weight = jnp.where(quad == j, weight_ref[lead, q % capacity], weight)
        for t in range(tile_count):
            masks[t].append(jnp.where(brick == t * QUADS + quad, weight, 0.0)[None])
    return masks


def tiles_of(field_ref):
    x_tiles = field_ref.shape[2] // LANES
    return [(y, x) for y in range(field_ref.shape[1] // EDGE) for x in range(x_tiles)]


STEP = 4
ROWS = STEP * EDGE // 8


def pack(field_ref, brick_ref, weight_ref, lead, out_ref):
    capacity = brick_ref.shape[1]
    depth = EDGE * capacity // QUADS
    parts = range(QUADS // capacity)
    tiles = tiles_of(field_ref)
    masks = [masks_of(brick_ref, weight_ref, lead, -1, part, len(tiles)) for part in parts]

    def body(i, carry):
        z = i * STEP
        sums = [None] * QUADS
        for part in parts:
            for t, (y, x) in enumerate(tiles):
                cells = field_ref[pl.ds(part * depth + z, STEP), pl.ds(y * EDGE, EDGE), pl.ds(x * LANES, LANES)]
                cells = cells.reshape(ROWS, 8, LANES)
                for r in range(QUADS):
                    term = masks[part][t][r] * cells
                    sums[r] = term if sums[r] is None else sums[r] + term
        total = sums[0]
        for r in range(1, QUADS):
            total = total + pltpu.roll(sums[r], r * EDGE, 2)
        out_ref[lead, pl.ds(z, STEP)] = total.reshape(STEP, EDGE, LANES)
        return carry

    lax.fori_loop(0, depth // STEP, body, 0)


def accumulate(got_ref, brick_ref, weight_ref, lead, sum_ref):
    capacity = brick_ref.shape[1]
    depth = EDGE * capacity // QUADS
    parts = range(QUADS // capacity)
    tiles = tiles_of(sum_ref)
    masks = [masks_of(brick_ref, weight_ref, lead, 1, part, len(tiles)) for part in parts]

    def body(i, carry):
        z = i * STEP
        cells = got_ref[lead, pl.ds(z, STEP)].reshape(ROWS, 8, LANES)
        turned = [cells] + [pltpu.roll(cells, r * EDGE, 2) for r in range(1, QUADS)]
        for part in parts:
            for t, (y, x) in enumerate(tiles):
                total = masks[part][t][0] * turned[0]
                for r in range(1, QUADS):
                    total = total + masks[part][t][r] * turned[r]
                at = (pl.ds(part * depth + z, STEP), pl.ds(y * EDGE, EDGE), pl.ds(x * LANES, LANES))
                sum_ref[at] = sum_ref[at] + total.reshape(STEP, EDGE, LANES)
        return carry

    lax.fori_loop(0, depth // STEP, body, 0)


def next_x(plane):
    lane = lax.broadcasted_iota(jnp.int32, plane.shape, 1)
    last = plane.shape[1] - 1
    after = jnp.where(lane == last, 0.0, pltpu.roll(plane, last, 1))
    before = jnp.where(lane == 0, 0.0, pltpu.roll(plane, 1, 1))
    return before, after


def next_y(plane, low, high):
    row = lax.broadcasted_iota(jnp.int32, plane.shape, 0)
    last = plane.shape[0] - 1
    after = jnp.where(row == last, high, pltpu.roll(plane, last, 0))
    before = jnp.where(row == 0, low, pltpu.roll(plane, 1, 0))
    return before, after


def partner(me, offset, count):
    other, bit = 0, 1
    while bit < count:
        other = other + ((me // bit + (offset // bit) % 2) % 2) * bit
        bit = bit * 2
    return other


def ring(axis):
    me, count = lax.axis_index(axis), lax.axis_size(axis)
    return (me + count - 1) % count, (me + 1) % count


def meet(count):
    barrier = pltpu.get_barrier_semaphore()
    me = lax.axis_index("slab")

    def greet(j, carry):
        other = partner(me, j, count)
        pl.semaphore_signal(barrier, inc=1, device_id={"slab": other}, device_id_type=MESH)
        return carry

    lax.fori_loop(1, count, greet, 0)
    for other in ring("pencil"):
        pl.semaphore_signal(barrier, inc=1, device_id={"pencil": other}, device_id_type=MESH)
    pl.semaphore_wait(barrier, count - 1 + 2)


def send(src, dst, sems, i, axis, other):
    return pltpu.make_async_remote_copy(
        src_ref=src, dst_ref=dst, send_sem=sems.at[0, i], recv_sem=sems.at[1, i],
        device_id={axis: other}, device_id_type=MESH,
    )


def swap(count, out_ref, got_ref, sems, fill, take):
    me = lax.axis_index("slab")

    def copy(j):
        other = partner(me, j, count)
        return other, send(out_ref.at[other], got_ref.at[me], sems, j, "slab", other)

    def start(i, carry):
        other, block = copy(count - 1 - i)
        fill(other)
        block.start()
        return carry

    lax.fori_loop(0, count - 1, start, 0)
    fill(me)
    take(out_ref, me)

    def finish(j, carry):
        other, block = copy(j)
        block.wait_recv()
        take(got_ref, other)
        return carry

    lax.fori_loop(1, count, finish, 0)

    def drain(j, carry):
        copy(j)[1].wait_send()
        return carry

    lax.fori_loop(1, count, drain, 0)


def forward_kernel(
    count, ids_ref, brick_ref, weight_ref, tpl_ref, fixed_ref, vel_ref,
    miss_ref, tz_low, tz_high, vz_low, vz_high, ty_low, ty_high, vy_low, vy_high,
    out_ref, got_ref, sems, halo_sems,
):
    z_cells, y_cells, _ = tpl_ref.shape
    meet(count)
    below, above = ring("slab")
    left, right = ring("pencil")
    z_last, y_last = pl.ds(z_cells - 1, 1), pl.ds(y_cells - 8, 8)
    z_head, y_head = pl.ds(0, 1), pl.ds(0, 8)
    halos = [
        send(tpl_ref.at[z_last], tz_low, halo_sems, 0, "slab", above),
        send(tpl_ref.at[z_head], tz_high, halo_sems, 1, "slab", below),
        send(vel_ref.at[:, z_last], vz_low, halo_sems, 2, "slab", above),
        send(vel_ref.at[:, z_head], vz_high, halo_sems, 3, "slab", below),
        send(tpl_ref.at[:, y_last], ty_low, halo_sems, 4, "pencil", right),
        send(tpl_ref.at[:, y_head], ty_high, halo_sems, 5, "pencil", left),
        send(vel_ref.at[:, :, y_last], vy_low, halo_sems, 6, "pencil", right),
        send(vel_ref.at[:, :, y_head], vy_high, halo_sems, 7, "pencil", left),
    ]
    for halo in halos:
        halo.start()
    miss_ref[...] = -fixed_ref[...]
    swap(
        count, out_ref, got_ref, sems,
        lambda other: pack(tpl_ref, ids_ref, None, other, out_ref),
        lambda ref, other: accumulate(ref, brick_ref, weight_ref, other, miss_ref),
    )
    for halo in halos:
        halo.wait()


def backward_kernel(
    count, ids_ref, brick_ref, weight_ref, miss_ref, tpl_ref, tz_low, tz_high, ty_low, ty_high,
    force_ref, fz_low, fz_high, fy_low, fy_high,
    out_ref, got_ref, sum_ref, head_ref, tail_ref, sems, halo_sems,
):
    z_cells, y_cells, _ = tpl_ref.shape
    meet(count)
    sum_ref[...] = jnp.zeros_like(sum_ref)
    swap(
        count, out_ref, got_ref, sems,
        lambda other: pack(miss_ref, brick_ref, weight_ref, other, out_ref),
        lambda ref, other: accumulate(ref, ids_ref, None, other, sum_ref),
    )
    slab, pencil = lax.axis_index("slab"), lax.axis_index("pencil")
    keep_below = jnp.where(slab == 0, 0.0, 1.0)
    keep_above = jnp.where(slab == count - 1, 0.0, 1.0)
    keep_left = jnp.where(pencil == 0, 0.0, 1.0)
    keep_right = jnp.where(pencil == lax.axis_size("pencil") - 1, 0.0, 1.0)

    def plane(z, below, above):
        here = tpl_ref[z]
        half = 0.5 * sum_ref[z]
        before_y, after_y = next_y(here, keep_left * ty_low[z, 7:8], keep_right * ty_high[z, 0:1])
        before_x, after_x = next_x(here)
        for c, slope in enumerate((above - below, after_y - before_y, after_x - before_x)):
            force = half * slope
            force_ref[c, z] = force
            head_ref[c, pl.ds(z, 1)] = force[0:1]
            tail_ref[c, pl.ds(z, 1)] = force[y_cells - 1:y_cells]

    plane(0, keep_below * tz_low[0], tpl_ref[1])
    plane(z_cells - 1, tpl_ref[z_cells - 2], keep_above * tz_high[0])
    below, above = ring("slab")
    left, right = ring("pencil")
    halos = [
        send(force_ref.at[:, pl.ds(z_cells - 1, 1)], fz_low, halo_sems, 0, "slab", above),
        send(force_ref.at[:, pl.ds(0, 1)], fz_high, halo_sems, 1, "slab", below),
        send(tail_ref, fy_low, halo_sems, 2, "pencil", right),
        send(head_ref, fy_high, halo_sems, 3, "pencil", left),
    ]
    halos[0].start()
    halos[1].start()

    def inner(z, carry):
        plane(z, tpl_ref[z - 1], tpl_ref[z + 1])
        return carry

    lax.fori_loop(1, z_cells - 1, inner, 0)
    halos[2].start()
    halos[3].start()
    for halo in halos:
        halo.wait()


def gradient_kernel(
    vel_ref, vel_before_ref, vel_after_ref, vz_low_ref, vz_high_ref, vy_low_ref, vy_high_ref,
    frc_ref, frc_before_ref, frc_after_ref, fz_low_ref, fz_high_ref, fy_low_ref, fy_high_ref, out_ref,
):
    block = pl.program_id(0)
    blocks = pl.num_programs(0)
    planes = vel_ref.shape[1]

    slab, pencil = lax.axis_index("slab"), lax.axis_index("pencil")
    keep_below = jnp.where(slab == 0, 0.0, 1.0)
    keep_above = jnp.where(slab == lax.axis_size("slab") - 1, 0.0, 1.0)
    keep_left = jnp.where(pencil == 0, 0.0, 1.0)
    keep_right = jnp.where(pencil == lax.axis_size("pencil") - 1, 0.0, 1.0)

    def around(ref, before_ref, after_ref, low_ref, high_ref, y_low, y_high, c, z):
        here = ref[c, z]
        if z == 0:
            below = jnp.where(block == 0, keep_below * low_ref[c, 0], before_ref[c, 0])
        else:
            below = ref[c, z - 1]
        if z == planes - 1:
            above = jnp.where(block == blocks - 1, keep_above * high_ref[c, 0], after_ref[c, 0])
        else:
            above = ref[c, z + 1]
        before_y, after_y = next_y(here, keep_left * y_low, keep_right * y_high)
        before_x, after_x = next_x(here)
        return here, below, above, before_y, after_y, before_x, after_x

    for z in range(planes):
        half = [0.5 * time_step * vel_ref[i, z] for i in range(3)]
        for c in range(3):
            v = around(vel_ref, vel_before_ref, vel_after_ref, vz_low_ref, vz_high_ref, vy_low_ref[c, z, 7:8], vy_high_ref[c, z, 0:1], c, z)
            laplace = 6.0 * v[0] - (((v[1] + v[2]) + (v[3] + v[4])) + (v[5] + v[6]))
            f = around(frc_ref, frc_before_ref, frc_after_ref, fz_low_ref, fz_high_ref, fy_low_ref[c, z:z + 1], fy_high_ref[c, z:z + 1], c, z)
            advect = half[0] * (f[2] - f[1]) + half[1] * (f[4] - f[3]) + half[2] * (f[6] - f[5])
            out_ref[c, z] = smooth_weight * laplace + f[0] - advect


def per_device(template, fixed_image, velocity, src_owner, src_local, weights):
    slab_count = lax.axis_size("slab")
    bricks, picks = src_owner.shape
    capacity = max(2, bricks * picks // slab_count)
    z_cells, y_cells, x_cells = template.shape
    depth = EDGE * capacity // QUADS
    f32, i32 = jnp.float32, jnp.int32
    smem = whole(pltpu.SMEM)
    table = (slab_count, capacity)

    ids, brick_of, slot_weight = pl.pallas_call(
        slots_kernel,
        out_shape=(
            jax.ShapeDtypeStruct(table, i32),
            jax.ShapeDtypeStruct(table, i32),
            jax.ShapeDtypeStruct(table, f32),
        ),
        in_specs=[smem] * 3,
        out_specs=(smem,) * 3,
        scratch_shapes=[pltpu.SMEM((slab_count,), i32)],
        name="slots",
    )(src_owner, src_local, weights)
    requested = lax.all_to_all(ids, "slab", split_axis=0, concat_axis=0, tiled=True)

    packed = (slab_count, depth, EDGE, LANES)
    z_face, y_face = (1, y_cells, x_cells), (z_cells, 8, x_cells)
    shapes = [template.shape, z_face, z_face, (3,) + z_face, (3,) + z_face]
    shapes += [y_face, y_face, (3,) + y_face, (3,) + y_face]
    sems = [pltpu.SemaphoreType.DMA((2, slab_count)), pltpu.SemaphoreType.DMA((2, 8))]
    miss, tz_low, tz_high, vz_low, vz_high, ty_low, ty_high, vy_low, vy_high = pl.pallas_call(
        functools.partial(forward_kernel, slab_count),
        out_shape=[jax.ShapeDtypeStruct(shape, f32) for shape in shapes],
        in_specs=[smem] * 3 + [whole(), whole(), whole(pl.ANY)],
        out_specs=[whole()] + [whole(pl.ANY)] * 8,
        scratch_shapes=[pltpu.VMEM(packed, f32), pltpu.VMEM(packed, f32)] + sems,
        compiler_params=params(collective_id=1, has_side_effects=True),
        name="forward",
    )(requested, brick_of, slot_weight, template, fixed_image, velocity)

    shapes = [(3,) + template.shape, (3,) + z_face, (3,) + z_face, (3, z_cells, x_cells), (3, z_cells, x_cells)]
    edge = pltpu.VMEM((3, z_cells, x_cells), f32)
    force, fz_low, fz_high, fy_low, fy_high = pl.pallas_call(
        functools.partial(backward_kernel, slab_count),
        out_shape=[jax.ShapeDtypeStruct(shape, f32) for shape in shapes],
        in_specs=[smem] * 3 + [whole()] * 6,
        out_specs=[whole()] + [whole(pl.ANY)] * 4,
        scratch_shapes=[pltpu.VMEM(packed, f32), pltpu.VMEM(packed, f32), pltpu.VMEM(template.shape, f32), edge, edge] + sems,
        compiler_params=params(collective_id=2, has_side_effects=True),
        name="backward",
    )(requested, brick_of, slot_weight, miss, template, tz_low, tz_high, ty_low, ty_high)

    rows = 8
    last = z_cells - 1
    block = (3, rows, y_cells, x_cells)
    plane = (3, 1, y_cells, x_cells)
    z_spec = pl.BlockSpec(plane, lambda z: (0, 0, 0, 0))
    field_specs = [
        pl.BlockSpec(block, lambda z: (0, z, 0, 0)),
        pl.BlockSpec(plane, lambda z: (0, jnp.maximum(z * rows - 1, 0), 0, 0)),
        pl.BlockSpec(plane, lambda z: (0, jnp.minimum(z * rows + rows, last), 0, 0)),
        z_spec,
        z_spec,
    ]
    vy_spec = pl.BlockSpec((3, rows, 8, x_cells), lambda z: (0, z, 0, 0))
    fy_spec = pl.BlockSpec((3, rows, x_cells), lambda z: (0, z, 0))
    return pl.pallas_call(
        gradient_kernel,
        grid=(z_cells // rows,),
        out_shape=jax.ShapeDtypeStruct(velocity.shape, f32),
        in_specs=field_specs + [vy_spec] * 2 + field_specs + [fy_spec] * 2,
        out_specs=pl.BlockSpec(block, lambda z: (0, z, 0, 0)),
        compiler_params=params(),
        name="gradient",
    )(
        velocity, velocity, velocity, vz_low, vz_high, vy_low, vy_high,
        force, force, force, fz_low, fz_high, fy_low, fy_high,
    )


def solution(mesh):
    in_specs = (
        P("slab", "pencil", None),
        P("slab", "pencil", None),
        P(None, "slab", "pencil", None),
        P(("slab", "pencil"), None),
        P(("slab", "pencil"), None),
        P(("slab", "pencil"), None),
    )
    out_specs = P(None, "slab", "pencil", None)
    return jax.shard_map(
        per_device, mesh=mesh, in_specs=in_specs, out_specs=out_specs, check_vma=False
    )
```

profile of v0, /device:TPU:0, one launch (start us, length us, event | category | flops | bytes accessed | tf_op | source)
XLA Modules:
  0.0 168.7 jit_solution(14851528230323115238)
XLA Ops:
  0.0 1.4 copy.13.owner_ref
  1.4 1.4 copy.14.local_ref
  2.7 1.3 copy.15.weight_ref
  4.1 2.2 %slots.1 = (s32[8,4]{1,0:T(8,128)}, s32[8,4]{1,0:T(8,128)}, f32[8,4]{1,0:T(8,128)}) custom-call(s32[16,2]{1,0:T(8,128)} %copy.13.owner_ref, s32[16,2]{1,0:T(8,128)} %copy.14.local_ref, f32[16,2]{1,0:T(8,128)} %copy.15.weight_ref), custom_call_target="tpu_custom_call" | custom-call | tf_op jit(solution)/shard_map/slots/pallas_call | solution.py:349
  6.3 0.0 copy-start.3
  6.3 9.8 %all_to_all.11 = s32[8,1,4]{2,1,0:T(1,128)S(1)} all-to-all(s32[8,1,4]{2,1,0:T(1,128)} %bitcast.6), channel_id=1, replica_groups=mesh['slab'=8,'pencil'=4] {'slab'}, dimensions={0} | all-to-all | bytes 256 | tf_op jit(solution)/shard_map/all_to_all | solution.py:361
  16.1 0.0 copy-start.1
  16.1 0.7 copy-done.1
  16.8 0.0 copy-start.2
  16.8 0.7 copy-done.2
  17.5 66.1 %forward.1 = (f32[32,64,256]{2,1,0:T(8,128)}, f32[1,64,256]{2,1,0:T(8,128)S(1)}, f32[1,64,256]{2,1,0:T(8,128)S(1)}, f32[3,1,64,256]{3,2,1,0:T(8,128)S(1)}, f32[3...) custom-call(s32[8,4]{1,0:T(8,128)S(1)} %bitcast.4, ...), custom_call_target="tpu_custom_call" | custom-call | tf_op jit(solution)/shard_map/forward/pallas_call | solution.py:368
  83.5 0.0 copy-done.3
  83.6 0.0 copy-start
  83.6 1.6 copy-done
  85.1 70.5 %backward.1 = (f32[3,32,64,256]{3,2,1,0:T(8,128)}, f32[3,1,64,256]{3,2,1,0:T(8,128)S(1)}, f32[3,1,64,256]{3,2,1,0:T(8,128)S(1)}, f32[3,32,256]{2,1,0:T(8,128)S(1)}, f32[3,32,256]{2,1,0:T(8,128)S(1)}) custom-call(s32[8,4]{1,0:T(8,128)S(1)} %bitcast.5, s32[8,4]{1,0:T(8,128)S(1)} %copy-done.1, f32[8,4]{1,0:T(8,128)S(1)} %copy-done.3, ...), custom_call_target="tpu_custom_call" | custom-call | tf_op jit(solution)/shard_map/backward/pallas_call | solution.py:380
  155.7 13.0 %gradient.1 = f32[3,32,64,256]{3,2,1,0:T(8,128)} custom-call(f32[3,32,64,256]{3,2,1,0:T(8,128)} %vel_after_ref.1, f32[3,32,64,256]{3,2,1,0:T(8,128)} %vel_after_ref.1, f32[3,32,64,256]{3,2,1,0:T(8,128)} %vel_after_ref.1, f32[3,1,64,256]{3,2,1,0:T(8,128)S(1)} %get-tuple-element.25.vz_low_ref, f32[3,1,64,256]{3,2,1,0:T(8,128)S(1)} %get-tuple-element.26.vz_high_ref, ...), custom_call_target="tpu_custom_call" | custom-call | tf_op jit(solution)/shard_map/gradient/pallas_call | solution.py:404
Async XLA Ops:
  6.3 77.3 %copy-start.3 = (f32[8,4]{1,0:T(8,128)S(1)}, f32[8,4]{1,0:T(8,128)}, u32[]{:S(2)}) copy-start(f32[8,4]{1,0:T(8,128)} %get-tuple-element.24.weight_ref) | copy-start | bytes 388
  16.1 0.7 copy-start.1
  16.8 0.7 copy-start.2
  83.6 1.6 copy-start
where the time goes:
time: 169 us
  Pallas kernels  152 us (90%)
  blocking collectives  9.83 us (6%)
  local copies, waits for them, and re-layouts  6.98 us (4%)
    pallas_call x1, Pallas kernels, per_device(): pl.pallas_call(functools.partial(backward_kernel, slab_count), out_shape=...  70.5 us
    pallas_call x1, Pallas kernels, per_device(): pl.pallas_call(functools.partial(forward_kernel, slab_count), out_shape=[...  66.1 us
    pallas_call x1, Pallas kernels, per_device(): pl.pallas_call(gradient_kernel, grid=(z_cells // rows,), out_shape=jax.Sh...  13 us
    all_to_all x1, blocking collectives, per_device(): lax.all_to_all(ids, 'slab', split_axis=0, concat_axis=0, tiled=True)  9.83 us
    unnamed x11, local copies, waits for them, and re-layouts  6.98 us

commit v1 on v0

--- a/solution.py
+++ b/solution.py
@@ -11,7 +11,8 @@
 LANES = 128
 QUADS = LANES // EDGE
 MESH = pl.DeviceIdType.MESH
-LIMIT = 50 * 1024 * 1024
+LIMIT = 56 * 1024 * 1024
+CHUNKS = 4
 
 smooth_weight = 0.1
 time_step = 0.5
@@ -25,7 +26,13 @@
     return pltpu.CompilerParams(vmem_limit_bytes=LIMIT, **kw)
 
 
-def slots_kernel(owner_ref, local_ref, weight_ref, ids_ref, brick_ref, slot_weight_ref, count_ref):
+def lane_quad():
+    return lax.broadcasted_iota(jnp.int32, (8, LANES), 1) // EDGE
+
+
+def slots_kernel(
+    owner_ref, local_ref, weight_ref, ids_out, brick_out, weight_out, ids_ref, brick_ref, slot_weight_ref, count_ref
+):
     readers, capacity = ids_ref.shape
     bricks, picks = owner_ref.shape
 
@@ -50,23 +57,33 @@
         return carry
 
     lax.fori_loop(0, bricks, place, 0)
-
-
-def masks_of(brick_ref, weight_ref, lead, sign, part, tile_count):
-    capacity = brick_ref.shape[1]
-    quad = lax.broadcasted_iota(jnp.int32, (8, LANES), 1) // EDGE
+    quad = lane_quad()
+
+    def spread(i, carry):
+        for ref, out in ((ids_ref, ids_out), (brick_ref, brick_out), (slot_weight_ref, weight_out)):
+            row = jnp.full((8, LANES), ref[i, 0])
+            for q in range(1, QUADS):
+                row = jnp.where(quad == q, ref[i, q % capacity], row)
+            out[i] = row
+        return carry
+
+    lax.fori_loop(0, readers, spread, 0)
+
+
+def masks_of(brick_ref, weight_ref, lead, sign, part, capacity, tile_count):
+    quad = lane_quad()
+    brick, weight = brick_ref[lead], jnp.ones((8, LANES), jnp.float32)
+    if weight_ref is not None:
+        weight = weight_ref[lead]
     masks = [[] for _ in range(tile_count)]
     for r in range(QUADS):
-        brick = jnp.full((8, LANES), -1, jnp.int32)
-        weight = jnp.ones((8, LANES), jnp.float32)
-        for j in range(QUADS):
-            q = (j - sign * r) % QUADS
-            if q // capacity == part:
-                brick = jnp.where(quad == j, brick_ref[lead, q % capacity], brick)
-                if weight_ref is not None:
-                    weight = jnp.where(quad == j, weight_ref[lead, q % capacity], weight)
+        turn = (sign * r % QUADS) * EDGE
+        here = pltpu.roll(brick, turn, 1) if turn else brick
+        scale = pltpu.roll(weight, turn, 1) if turn and weight_ref is not None else weight
+        if capacity < QUADS:
+            here = jnp.where((quad - sign * r + QUADS) % QUADS // capacity == part, here, -1)
         for t in range(tile_count):
-            masks[t].append(jnp.where(brick == t * QUADS + quad, weight, 0.0)[None])
+            masks[t].append(jnp.where(here == t * QUADS + quad, scale, 0.0)[None])
     return masks
 
 
@@ -79,15 +96,16 @@
 ROWS = STEP * EDGE // 8
 
 
-def pack(field_ref, brick_ref, weight_ref, lead, out_ref):
-    capacity = brick_ref.shape[1]
-    depth = EDGE * capacity // QUADS
+def pack(field_ref, brick_ref, weight_ref, lead, chunk, out_ref):
+    depth = out_ref.shape[1]
+    capacity = QUADS * depth // EDGE
     parts = range(QUADS // capacity)
+    size = depth // CHUNKS
     tiles = tiles_of(field_ref)
-    masks = [masks_of(brick_ref, weight_ref, lead, -1, part, len(tiles)) for part in parts]
+    masks = [masks_of(brick_ref, weight_ref, lead, -1, part, capacity, len(tiles)) for part in parts]
 
     def body(i, carry):
-        z = i * STEP
+        z = chunk * size + i * STEP
         sums = [None] * QUADS
         for part in parts:
             for t, (y, x) in enumerate(tiles):
@@ -102,18 +120,19 @@
         out_ref[lead, pl.ds(z, STEP)] = total.reshape(STEP, EDGE, LANES)
         return carry
 
-    lax.fori_loop(0, depth // STEP, body, 0)
-
-
-def accumulate(got_ref, brick_ref, weight_ref, lead, sum_ref):
-    capacity = brick_ref.shape[1]
-    depth = EDGE * capacity // QUADS
+    lax.fori_loop(0, size // STEP, body, 0)
+
+
+def accumulate(got_ref, brick_ref, weight_ref, lead, chunk, sum_ref):
+    depth = got_ref.shape[1]
+    capacity = QUADS * depth // EDGE
     parts = range(QUADS // capacity)
+    size = depth // CHUNKS
     tiles = tiles_of(sum_ref)
-    masks = [masks_of(brick_ref, weight_ref, lead, 1, part, len(tiles)) for part in parts]
+    masks = [masks_of(brick_ref, weight_ref, lead, 1, part, capacity, len(tiles)) for part in parts]
 
     def body(i, carry):
-        z = i * STEP
+        z = chunk * size + i * STEP
         cells = got_ref[lead, pl.ds(z, STEP)].reshape(ROWS, 8, LANES)
         turned = [cells] + [pltpu.roll(cells, r * EDGE, 2) for r in range(1, QUADS)]
         for part in parts:
@@ -125,7 +144,7 @@
                 sum_ref[at] = sum_ref[at] + total.reshape(STEP, EDGE, LANES)
         return carry
 
-    lax.fori_loop(0, depth // STEP, body, 0)
+    lax.fori_loop(0, size // STEP, body, 0)
 
 
 def next_x(plane):
@@ -179,49 +198,49 @@
     )
 
 
-def swap(count, out_ref, got_ref, sems, fill, take):
+def block(count, out_ref, got_ref, sems, chunk, j):
     me = lax.axis_index("slab")
-
-    def copy(j):
-        other = partner(me, j, count)
-        return other, send(out_ref.at[other], got_ref.at[me], sems, j, "slab", other)
-
-    def start(i, carry):
-        other, block = copy(count - 1 - i)
-        fill(other)
-        block.start()
-        return carry
-
-    lax.fori_loop(0, count - 1, start, 0)
-    fill(me)
-    take(out_ref, me)
-
-    def finish(j, carry):
-        other, block = copy(j)
-        block.wait_recv()
-        take(got_ref, other)
-        return carry
-
-    lax.fori_loop(1, count, finish, 0)
-
-    def drain(j, carry):
-        copy(j)[1].wait_send()
-        return carry
-
-    lax.fori_loop(1, count, drain, 0)
-
-
-def forward_kernel(
+    other = partner(me, j, count)
+    size = out_ref.shape[1] // CHUNKS
+    planes = pl.ds(chunk * size, size)
+    return other, send(
+        out_ref.at[other, planes], got_ref.at[me, planes], sems, chunk * count + j, "slab", other
+    )
+
+
+def main_kernel(
     count, ids_ref, brick_ref, weight_ref, tpl_ref, fixed_ref, vel_ref,
-    miss_ref, tz_low, tz_high, vz_low, vz_high, ty_low, ty_high, vy_low, vy_high,
-    out_ref, got_ref, sems, halo_sems,
+    force_ref, fz_low, fz_high, fy_low, fy_high, vz_low, vz_high, vy_low, vy_high,
+    want_ref, there_out, there_got, back_out, back_got, miss_ref, sum_ref,
+    tz_low, tz_high, ty_low, ty_high, head_ref, tail_ref,
+    want_sems, there_sems, back_sems, halo_sems, own_sem,
 ):
     z_cells, y_cells, _ = tpl_ref.shape
-    meet(count)
+    me = lax.axis_index("slab")
+    pencil = lax.axis_index("pencil")
+    depth = there_out.shape[1]
+    size = depth // CHUNKS
+    keep_below = jnp.where(me == 0, 0.0, 1.0)
+    keep_above = jnp.where(me == count - 1, 0.0, 1.0)
+    keep_left = jnp.where(pencil == 0, 0.0, 1.0)
+    keep_right = jnp.where(pencil == lax.axis_size("pencil") - 1, 0.0, 1.0)
     below, above = ring("slab")
     left, right = ring("pencil")
     z_last, y_last = pl.ds(z_cells - 1, 1), pl.ds(y_cells - 8, 8)
     z_head, y_head = pl.ds(0, 1), pl.ds(0, 8)
+    meet(count)
+
+    def want(j):
+        other = partner(me, j, count)
+        return other, send(ids_ref.at[other], want_ref.at[me], want_sems, j, "slab", other)
+
+    def ask(j, carry):
+        want(j)[1].start()
+        return carry
+
+    lax.fori_loop(1, count, ask, 0)
+    own = pltpu.make_async_copy(ids_ref.at[me], want_ref.at[me], own_sem)
+    own.start()
     halos = [
         send(tpl_ref.at[z_last], tz_low, halo_sems, 0, "slab", above),
         send(tpl_ref.at[z_head], tz_high, halo_sems, 1, "slab", below),
@@ -232,70 +251,109 @@
         send(vel_ref.at[:, :, y_last], vy_low, halo_sems, 6, "pencil", right),
         send(vel_ref.at[:, :, y_head], vy_high, halo_sems, 7, "pencil", left),
     ]
+    own.wait()
+
+    def heard(j, carry):
+        want(j)[1].wait()
+        return carry
+
+    lax.fori_loop(1, count, heard, 0)
+
+    def there(chunk, carry):
+        def start(i, inner):
+            other, copy = block(count, there_out, there_got, there_sems, chunk, count - 1 - i)
+            pack(tpl_ref, want_ref, None, other, chunk, there_out)
+            copy.start()
+            return inner
+
+        lax.fori_loop(0, count - 1, start, 0)
+        pack(tpl_ref, want_ref, None, me, chunk, there_out)
+        return carry
+
+    lax.fori_loop(0, CHUNKS, there, 0)
     for halo in halos:
         halo.start()
     miss_ref[...] = -fixed_ref[...]
-    swap(
-        count, out_ref, got_ref, sems,
-        lambda other: pack(tpl_ref, ids_ref, None, other, out_ref),
-        lambda ref, other: accumulate(ref, brick_ref, weight_ref, other, miss_ref),
-    )
+    sum_ref[...] = jnp.zeros_like(sum_ref)
+
+    def back(chunk, carry):
+        accumulate(there_out, brick_ref, weight_ref, me, chunk, miss_ref)
+
+        def finish(j, inner):
+            other, copy = block(count, there_out, there_got, there_sems, chunk, j)
+            copy.wait_recv()
+            accumulate(there_got, brick_ref, weight_ref, other, chunk, miss_ref)
+            return inner
+
+        lax.fori_loop(1, count, finish, 0)
+
+        def start(i, inner):
+            other, copy = block(count, back_out, back_got, back_sems, chunk, count - 1 - i)
+            pack(miss_ref, brick_ref, weight_ref, other, chunk, back_out)
+            copy.start()
+            return inner
+
+        lax.fori_loop(0, count - 1, start, 0)
+        pack(miss_ref, brick_ref, weight_ref, me, chunk, back_out)
+        accumulate(back_out, want_ref, None, me, chunk, sum_ref)
+        return carry
+
+    lax.fori_loop(0, CHUNKS, back, 0)
     for halo in halos:
         halo.wait()
 
-
-def backward_kernel(
-    count, ids_ref, brick_ref, weight_ref, miss_ref, tpl_ref, tz_low, tz_high, ty_low, ty_high,
-    force_ref, fz_low, fz_high, fy_low, fy_high,
-    out_ref, got_ref, sum_ref, head_ref, tail_ref, sems, halo_sems,
-):
-    z_cells, y_cells, _ = tpl_ref.shape
-    meet(count)
-    sum_ref[...] = jnp.zeros_like(sum_ref)
-    swap(
-        count, out_ref, got_ref, sems,
-        lambda other: pack(miss_ref, brick_ref, weight_ref, other, out_ref),
-        lambda ref, other: accumulate(ref, ids_ref, None, other, sum_ref),
-    )
-    slab, pencil = lax.axis_index("slab"), lax.axis_index("pencil")
-    keep_below = jnp.where(slab == 0, 0.0, 1.0)
-    keep_above = jnp.where(slab == count - 1, 0.0, 1.0)
-    keep_left = jnp.where(pencil == 0, 0.0, 1.0)
-    keep_right = jnp.where(pencil == lax.axis_size("pencil") - 1, 0.0, 1.0)
-
-    def plane(z, below, above):
+    def plane(z):
         here = tpl_ref[z]
+        before_z = jnp.where(z == 0, keep_below * tz_low[0], tpl_ref[jnp.maximum(z - 1, 0)])
+        after_z = jnp.where(z == z_cells - 1, keep_above * tz_high[0], tpl_ref[jnp.minimum(z + 1, z_cells - 1)])
         half = 0.5 * sum_ref[z]
         before_y, after_y = next_y(here, keep_left * ty_low[z, 7:8], keep_right * ty_high[z, 0:1])
         before_x, after_x = next_x(here)
-        for c, slope in enumerate((above - below, after_y - before_y, after_x - before_x)):
+        for c, slope in enumerate((after_z - before_z, after_y - before_y, after_x - before_x)):
             force = half * slope
             force_ref[c, z] = force
             head_ref[c, pl.ds(z, 1)] = force[0:1]
             tail_ref[c, pl.ds(z, 1)] = force[y_cells - 1:y_cells]
 
-    plane(0, keep_below * tz_low[0], tpl_ref[1])
-    plane(z_cells - 1, tpl_ref[z_cells - 2], keep_above * tz_high[0])
-    below, above = ring("slab")
-    left, right = ring("pencil")
-    halos = [
-        send(force_ref.at[:, pl.ds(z_cells - 1, 1)], fz_low, halo_sems, 0, "slab", above),
-        send(force_ref.at[:, pl.ds(0, 1)], fz_high, halo_sems, 1, "slab", below),
-        send(tail_ref, fy_low, halo_sems, 2, "pencil", right),
-        send(head_ref, fy_high, halo_sems, 3, "pencil", left),
+    def end(chunk, carry):
+        def finish(j, inner):
+            other, copy = block(count, back_out, back_got, back_sems, chunk, j)
+            copy.wait_recv()
+            accumulate(back_got, want_ref, None, other, chunk, sum_ref)
+            return inner
+
+        lax.fori_loop(1, count, finish, 0)
+        for part in range(EDGE // depth):
+
+            def step(i, inner, part=part):
+                plane(part * depth + chunk * size + i)
+                return inner
+
+            lax.fori_loop(0, size, step, 0)
+        return carry
+
+    lax.fori_loop(0, CHUNKS, end, 0)
+    faces = [
+        send(force_ref.at[:, z_last], fz_low, halo_sems, 8, "slab", above),
+        send(force_ref.at[:, z_head], fz_high, halo_sems, 9, "slab", below),
+        send(tail_ref, fy_low, halo_sems, 10, "pencil", right),
+        send(head_ref, fy_high, halo_sems, 11, "pencil", left),
     ]
-    halos[0].start()
-    halos[1].start()
-
-    def inner(z, carry):
-        plane(z, tpl_ref[z - 1], tpl_ref[z + 1])
-        return carry
-
-    lax.fori_loop(1, z_cells - 1, inner, 0)
-    halos[2].start()
-    halos[3].start()
-    for halo in halos:
-        halo.wait()
+    for face in faces:
+        face.start()
+
+    def drain(chunk, carry):
+        def finish(j, inner):
+            block(count, there_out, there_got, there_sems, chunk, j)[1].wait_send()
+            block(count, back_out, back_got, back_sems, chunk, j)[1].wait_send()
+            return inner
+
+        lax.fori_loop(1, count, finish, 0)
+        return carry
+
+    lax.fori_loop(0, CHUNKS, drain, 0)
+    for face in faces:
+        face.wait()
 
 
 def gradient_kernel(
@@ -345,47 +403,35 @@
     f32, i32 = jnp.float32, jnp.int32
     smem = whole(pltpu.SMEM)
     table = (slab_count, capacity)
+    spread = (slab_count, 8, LANES)
 
     ids, brick_of, slot_weight = pl.pallas_call(
         slots_kernel,
-        out_shape=(
-            jax.ShapeDtypeStruct(table, i32),
-            jax.ShapeDtypeStruct(table, i32),
-            jax.ShapeDtypeStruct(table, f32),
-        ),
+        out_shape=[jax.ShapeDtypeStruct(spread, kind) for kind in (i32, i32, f32)],
         in_specs=[smem] * 3,
-        out_specs=(smem,) * 3,
-        scratch_shapes=[pltpu.SMEM((slab_count,), i32)],
+        out_specs=[whole()] * 3,
+        scratch_shapes=[pltpu.SMEM(table, i32), pltpu.SMEM(table, i32), pltpu.SMEM(table, f32), pltpu.SMEM((slab_count,), i32)],
         name="slots",
     )(src_owner, src_local, weights)
-    requested = lax.all_to_all(ids, "slab", split_axis=0, concat_axis=0, tiled=True)
-
-    packed = (slab_count, depth, EDGE, LANES)
+
+    packed = pltpu.VMEM((slab_count, depth, EDGE, LANES), f32)
     z_face, y_face = (1, y_cells, x_cells), (z_cells, 8, x_cells)
-    shapes = [template.shape, z_face, z_face, (3,) + z_face, (3,) + z_face]
-    shapes += [y_face, y_face, (3,) + y_face, (3,) + y_face]
-    sems = [pltpu.SemaphoreType.DMA((2, slab_count)), pltpu.SemaphoreType.DMA((2, 8))]
-    miss, tz_low, tz_high, vz_low, vz_high, ty_low, ty_high, vy_low, vy_high = pl.pallas_call(
-        functools.partial(forward_kernel, slab_count),
+    edge = (3, z_cells, x_cells)
+    shapes = [(3,) + template.shape, (3,) + z_face, (3,) + z_face, edge, edge]
+    shapes += [(3,) + z_face, (3,) + z_face, (3,) + y_face, (3,) + y_face]
+    field = pltpu.VMEM(template.shape, f32)
+    block_sems = pltpu.SemaphoreType.DMA((2, CHUNKS * slab_count))
+    force, fz_low, fz_high, fy_low, fy_high, vz_low, vz_high, vy_low, vy_high = pl.pallas_call(
+        functools.partial(main_kernel, slab_count),
         out_shape=[jax.ShapeDtypeStruct(shape, f32) for shape in shapes],
-        in_specs=[smem] * 3 + [whole(), whole(), whole(pl.ANY)],
+        in_specs=[whole()] * 5 + [whole(pl.ANY)],
         out_specs=[whole()] + [whole(pl.ANY)] * 8,
-        scratch_shapes=[pltpu.VMEM(packed, f32), pltpu.VMEM(packed, f32)] + sems,
+        scratch_shapes=[pltpu.VMEM(spread, i32)] + [packed] * 4 + [field] * 2
+        + [pltpu.VMEM(z_face, f32)] * 2 + [pltpu.VMEM(y_face, f32)] * 2 + [pltpu.VMEM(edge, f32)] * 2
+        + [pltpu.SemaphoreType.DMA((2, slab_count)), block_sems, block_sems, pltpu.SemaphoreType.DMA((2, 12)), pltpu.SemaphoreType.DMA],
         compiler_params=params(collective_id=1, has_side_effects=True),
-        name="forward",
-    )(requested, brick_of, slot_weight, template, fixed_image, velocity)
-
-    shapes = [(3,) + template.shape, (3,) + z_face, (3,) + z_face, (3, z_cells, x_cells), (3, z_cells, x_cells)]
-    edge = pltpu.VMEM((3, z_cells, x_cells), f32)
-    force, fz_low, fz_high, fy_low, fy_high = pl.pallas_call(
-        functools.partial(backward_kernel, slab_count),
-        out_shape=[jax.ShapeDtypeStruct(shape, f32) for shape in shapes],
-        in_specs=[smem] * 3 + [whole()] * 6,
-        out_specs=[whole()] + [whole(pl.ANY)] * 4,
-        scratch_shapes=[pltpu.VMEM(packed, f32), pltpu.VMEM(packed, f32), pltpu.VMEM(template.shape, f32), edge, edge] + sems,
-        compiler_params=params(collective_id=2, has_side_effects=True),
-        name="backward",
-    )(requested, brick_of, slot_weight, miss, template, tz_low, tz_high, ty_low, ty_high)
+        name="transport",
+    )(ids, brick_of, slot_weight, template, fixed_image, velocity)
 
     rows = 8
     last = z_cells - 1

time: 169 us -> 142 us (0.84)
  Pallas kernels: 152 us -> 137 us
  blocking collectives: 9.83 us -> 0 us
  local copies, waits for them, and re-layouts: 6.98 us -> 4.04 us
    pallas_call x3 -> x2, Pallas kernels: 139 us -> 124 us  [the longest x1 122 us: per_device(): pl.pallas_call(functools.partial(main_kernel, slab_count), out_shape=[jax...]
    all_to_all x1 -> x0, blocking collectives: 9.83 us -> none  [per_device(): lax.all_to_all(ids, 'slab', split_axis=0, concat_axis=0, tiled=True)]
    unnamed x11 -> x3, local copies, waits for them, and re-layouts: 6.98 us -> 4.04 us
where the time goes in v1:
time: 142 us; the launch traced here: 141 us
  Pallas kernels  137 us (96%)
  local copies, waits for them, and re-layouts  4.04 us (3%)
    pallas_call x1, Pallas kernels, per_device(): pl.pallas_call(functools.partial(main_kernel, slab_count), out_shape=[jax...  122 us
    pallas_call x1, Pallas kernels, per_device(): pl.pallas_call(gradient_kernel, grid=(z_cells // rows,), out_shape=jax.Sh...  13.5 us
    unnamed x3, local copies, waits for them, and re-layouts  4.04 us

profile of v1, /device:TPU:0, one launch (start us, length us, event | category | flops | bytes accessed | tf_op | source)
XLA Modules:
  0.0 141.4 jit_solution(17967682650032068542)
XLA Ops:
  0.0 1.3 copy.7.owner_ref
  1.3 1.3 copy.8.local_ref
  2.7 1.3 copy.9.weight_ref
  4.0 2.2 %slots.1 = (s32[8,8,128]{2,1,0:T(8,128)}, s32[8,8,128]{2,1,0:T(8,128)}, f32[8,8,128]{2,1,0:T(8,128)}) custom-call(s32[16,2]{1,0:T(8,128)} %copy.7.owner_ref, s32[16,2]{1,0:T(8,128)} %copy.8.local_ref, f32[16,2]{1,0:T(8,128)} %copy.9.weight_ref), custom_call_target="tpu_custom_call" | custom-call | tf_op jit(solution)/shard_map/slots/pallas_call | solution.py:408
  6.3 121.6 %transport.1 = (f32[3,32,64,256]{3,2,1,0:T(8,128)}, f32[3,1,64,256]{3,2,1,0:T(8,128)}, f32[3,1,64,256]{3,2,1,0:T(8,128)}, f32[3,32,256]{2,1,0:T(8,128)}, f32[3,3...) custom-call(s32[8,8,128]{2,1,0:T(8,128)} %get-tuple-element.17.ids_r, ...), custom_call_target="tpu_custom_call" | custom-call | tf_op jit(solution)/shard_map/transport/pallas_call | solution.py:424
  127.9 13.5 %gradient.1 = f32[3,32,64,256]{3,2,1,0:T(8,128)} custom-call(f32[3,32,64,256]{3,2,1,0:T(8,128)} %vel_after_ref.1, f32[3,32,64,256]{3,2,1,0:T(8,128)} %vel_after_ref.1, f32[3,32,64,256]{3,2,1,0:T(8,128)} %vel_after_ref.1, f32[3,1,64,256]{3,2,1,0:T(8,128)} %get-tuple-element.20.vz_low_ref, f32[3,1,64,256]{3,2,1,0:T(8,128)} %get-tuple-element.21.vz_high_ref, ...), custom_call_target="tpu_custom_call" | custom-call | tf_op jit(solution)/shard_map/gradient/pallas_call | solution.py:450

commit v2 on v1

--- a/solution.py
+++ b/solution.py
@@ -34,7 +34,7 @@
     owner_ref, local_ref, weight_ref, ids_out, brick_out, weight_out, ids_ref, brick_ref, slot_weight_ref, count_ref
 ):
     readers, capacity = ids_ref.shape
-    bricks, picks = owner_ref.shape
+    picks, bricks = owner_ref.shape
 
     def clear(i, carry):
         count_ref[i] = 0
@@ -48,12 +48,12 @@
 
     def place(g, carry):
         for k in range(picks):
-            owner = owner_ref[g, k]
+            owner = owner_ref[k, g]
             slot = count_ref[owner]
             count_ref[owner] = slot + 1
-            ids_ref[owner, slot] = local_ref[g, k]
+            ids_ref[owner, slot] = local_ref[k, g]
             brick_ref[owner, slot] = g
-            slot_weight_ref[owner, slot] = weight_ref[g, k]
+            slot_weight_ref[owner, slot] = weight_ref[k, g]
         return carry
 
     lax.fori_loop(0, bricks, place, 0)
@@ -198,6 +198,10 @@
     )
 
 
+def turn_of(turn):
+    return (turn * (CHUNKS - 1)) % CHUNKS
+
+
 def block(count, out_ref, got_ref, sems, chunk, j):
     me = lax.axis_index("slab")
     other = partner(me, j, count)
@@ -211,9 +215,9 @@
 def main_kernel(
     count, ids_ref, brick_ref, weight_ref, tpl_ref, fixed_ref, vel_ref,
     force_ref, fz_low, fz_high, fy_low, fy_high, vz_low, vz_high, vy_low, vy_high,
-    want_ref, there_out, there_got, back_out, back_got, miss_ref, sum_ref,
+    want_ref, there_out, there_got, back_out, back_got, miss_ref, sum_ref, total_ref,
     tz_low, tz_high, ty_low, ty_high, head_ref, tail_ref,
-    want_sems, there_sems, back_sems, halo_sems, own_sem,
+    want_sems, there_sems, back_sems, halo_sems, store_sems, own_sem, fixed_sem,
 ):
     z_cells, y_cells, _ = tpl_ref.shape
     me = lax.axis_index("slab")
@@ -228,6 +232,8 @@
     left, right = ring("pencil")
     z_last, y_last = pl.ds(z_cells - 1, 1), pl.ds(y_cells - 8, 8)
     z_head, y_head = pl.ds(0, 1), pl.ds(0, 8)
+    fixed = pltpu.make_async_copy(fixed_ref, miss_ref, fixed_sem)
+    fixed.start()
     meet(count)
 
     def want(j):
@@ -251,6 +257,11 @@
         send(vel_ref.at[:, :, y_last], vy_low, halo_sems, 6, "pencil", right),
         send(vel_ref.at[:, :, y_head], vy_high, halo_sems, 7, "pencil", left),
     ]
+    for halo in halos:
+        halo.start()
+    sum_ref[...] = jnp.zeros_like(sum_ref)
+    fixed.wait()
+    miss_ref[...] = -miss_ref[...]
     own.wait()
 
     def heard(j, carry):
@@ -259,7 +270,9 @@
 
     lax.fori_loop(1, count, heard, 0)
 
-    def there(chunk, carry):
+    def there(turn, carry):
+        chunk = turn_of(turn)
+
         def start(i, inner):
             other, copy = block(count, there_out, there_got, there_sems, chunk, count - 1 - i)
             pack(tpl_ref, want_ref, None, other, chunk, there_out)
@@ -271,12 +284,9 @@
         return carry
 
     lax.fori_loop(0, CHUNKS, there, 0)
-    for halo in halos:
-        halo.start()
-    miss_ref[...] = -fixed_ref[...]
-    sum_ref[...] = jnp.zeros_like(sum_ref)
-
-    def back(chunk, carry):
+
+    def back(turn, carry):
+        chunk = turn_of(turn)
         accumulate(there_out, brick_ref, weight_ref, me, chunk, miss_ref)
 
         def finish(j, inner):
@@ -311,11 +321,18 @@
         before_x, after_x = next_x(here)
         for c, slope in enumerate((after_z - before_z, after_y - before_y, after_x - before_x)):
             force = half * slope
-            force_ref[c, z] = force
+            total_ref[c, z] = force
             head_ref[c, pl.ds(z, 1)] = force[0:1]
             tail_ref[c, pl.ds(z, 1)] = force[y_cells - 1:y_cells]
 
-    def end(chunk, carry):
+    def store(chunk, part):
+        planes = pl.ds(part * depth + chunk * size, size)
+        at = chunk * (EDGE // depth) + part
+        return pltpu.make_async_copy(total_ref.at[:, planes], force_ref.at[:, planes], store_sems.at[at])
+
+    def end(turn, carry):
+        chunk = turn_of(turn)
+
         def finish(j, inner):
             other, copy = block(count, back_out, back_got, back_sems, chunk, j)
             copy.wait_recv()
@@ -330,17 +347,21 @@
                 return inner
 
             lax.fori_loop(0, size, step, 0)
-        return carry
-
-    lax.fori_loop(0, CHUNKS, end, 0)
+            store(chunk, part).start()
+        return carry
+
+    lax.fori_loop(0, 2, end, 0)
     faces = [
-        send(force_ref.at[:, z_last], fz_low, halo_sems, 8, "slab", above),
-        send(force_ref.at[:, z_head], fz_high, halo_sems, 9, "slab", below),
+        send(total_ref.at[:, z_last], fz_low, halo_sems, 8, "slab", above),
+        send(total_ref.at[:, z_head], fz_high, halo_sems, 9, "slab", below),
         send(tail_ref, fy_low, halo_sems, 10, "pencil", right),
         send(head_ref, fy_high, halo_sems, 11, "pencil", left),
     ]
-    for face in faces:
-        face.start()
+    faces[0].start()
+    faces[1].start()
+    lax.fori_loop(2, CHUNKS, end, 0)
+    faces[2].start()
+    faces[3].start()
 
     def drain(chunk, carry):
         def finish(j, inner):
@@ -349,6 +370,8 @@
             return inner
 
         lax.fori_loop(1, count, finish, 0)
+        for part in range(EDGE // depth):
+            store(chunk, part).wait()
         return carry
 
     lax.fori_loop(0, CHUNKS, drain, 0)
@@ -412,7 +435,7 @@
         out_specs=[whole()] * 3,
         scratch_shapes=[pltpu.SMEM(table, i32), pltpu.SMEM(table, i32), pltpu.SMEM(table, f32), pltpu.SMEM((slab_count,), i32)],
         name="slots",
-    )(src_owner, src_local, weights)
+    )(src_owner.T, src_local.T, weights.T)
 
     packed = pltpu.VMEM((slab_count, depth, EDGE, LANES), f32)
     z_face, y_face = (1, y_cells, x_cells), (z_cells, 8, x_cells)
@@ -424,11 +447,12 @@
     force, fz_low, fz_high, fy_low, fy_high, vz_low, vz_high, vy_low, vy_high = pl.pallas_call(
         functools.partial(main_kernel, slab_count),
         out_shape=[jax.ShapeDtypeStruct(shape, f32) for shape in shapes],
-        in_specs=[whole()] * 5 + [whole(pl.ANY)],
-        out_specs=[whole()] + [whole(pl.ANY)] * 8,
-        scratch_shapes=[pltpu.VMEM(spread, i32)] + [packed] * 4 + [field] * 2
+        in_specs=[whole()] * 4 + [whole(pl.ANY)] * 2,
+        out_specs=[whole(pl.ANY)] * 9,
+        scratch_shapes=[pltpu.VMEM(spread, i32)] + [packed] * 4 + [field] * 2 + [pltpu.VMEM((3,) + template.shape, f32)]
         + [pltpu.VMEM(z_face, f32)] * 2 + [pltpu.VMEM(y_face, f32)] * 2 + [pltpu.VMEM(edge, f32)] * 2
-        + [pltpu.SemaphoreType.DMA((2, slab_count)), block_sems, block_sems, pltpu.SemaphoreType.DMA((2, 12)), pltpu.SemaphoreType.DMA],
+        + [pltpu.SemaphoreType.DMA((2, slab_count)), block_sems, block_sems, pltpu.SemaphoreType.DMA((2, 12))]
+        + [pltpu.SemaphoreType.DMA((CHUNKS * (EDGE // depth),)), pltpu.SemaphoreType.DMA, pltpu.SemaphoreType.DMA],
         compiler_params=params(collective_id=1, has_side_effects=True),
         name="transport",
     )(ids, brick_of, slot_weight, template, fixed_image, velocity)

time: 142 us -> 131 us (0.923)
  Pallas kernels: 137 us -> 131 us
  local copies, waits for them, and re-layouts: 4.04 us -> 0 us
    pallas_call x1, Pallas kernels: 122 us -> 115 us  [per_device(): pl.pallas_call(functools.partial(main_kernel, slab_count), out_shape=[jax...]
    unnamed x3 -> x0, local copies, waits for them, and re-layouts: 4.04 us -> none
where the time goes in v2:
time: 131 us
  Pallas kernels  131 us (100%)
    pallas_call x1, Pallas kernels, per_device(): pl.pallas_call(functools.partial(main_kernel, slab_count), out_shape=[jax...  115 us
    pallas_call x1, Pallas kernels, per_device(): pl.pallas_call(gradient_kernel, grid=(z_cells // rows,), out_shape=jax.Sh...  13.5 us

profile of v2, /device:TPU:0, one launch (start us, length us, event | category | flops | bytes accessed | tf_op | source)
XLA Modules:
  0.0 130.8 jit_solution(7076924033821016700)
XLA Ops:
  0.0 1.9 %slots.1 = (s32[8,8,128]{2,1,0:T(8,128)}, s32[8,8,128]{2,1,0:T(8,128)}, f32[8,8,128]{2,1,0:T(8,128)}) custom-call(s32[2,16]{1,0:T(2,128)} %bitcast.3, s32[2,16]{1,0:T(2,128)} %bitcast.4, f32[2,16]{1,0:T(2,128)} %bitcast.5), custom_call_target="tpu_custom_call" | custom-call | tf_op jit(solution)/shard_map/slots/pallas_call | solution.py:431
  1.9 115.4 %transport.1 = (f32[3,32,64,256]{3,2,1,0:T(8,128)}, f32[3,1,64,256]{3,2,1,0:T(8,128)}, f32[3,1,64,256]{3,2,1,0:T(8,128)}, f32[3,32,256]{2,1,0:T(8,128)}, f32[3,3...) custom-call(s32[8,8,128]{2,1,0:T(8,128)} %get-tuple-element.17.ids_r, ...), custom_call_target="tpu_custom_call" | custom-call | tf_op jit(solution)/shard_map/transport/pallas_call | solution.py:447
  117.3 13.5 %gradient.1 = f32[3,32,64,256]{3,2,1,0:T(8,128)} custom-call(f32[3,32,64,256]{3,2,1,0:T(8,128)} %vel_after_ref.1, f32[3,32,64,256]{3,2,1,0:T(8,128)} %vel_after_ref.1, f32[3,32,64,256]{3,2,1,0:T(8,128)} %vel_after_ref.1, f32[3,1,64,256]{3,2,1,0:T(8,128)} %get-tuple-element.20.vz_low_ref, f32[3,1,64,256]{3,2,1,0:T(8,128)} %get-tuple-element.21.vz_high_ref, ...), custom_call_target="tpu_custom_call" | custom-call | tf_op jit(solution)/shard_map/gradient/pallas_call | solution.py:474

commit v3 on v2

--- a/solution.py
+++ b/solution.py
@@ -214,10 +214,11 @@
 
 def main_kernel(
     count, ids_ref, brick_ref, weight_ref, tpl_ref, fixed_ref, vel_ref,
-    force_ref, fz_low, fz_high, fy_low, fy_high, vz_low, vz_high, vy_low, vy_high,
+    force_ref, base_ref, fz_low, fz_high, fy_low, fy_high,
     want_ref, there_out, there_got, back_out, back_got, miss_ref, sum_ref, total_ref,
+    speed_ref, vz_low, vz_high, vy_low, vy_high,
     tz_low, tz_high, ty_low, ty_high, head_ref, tail_ref,
-    want_sems, there_sems, back_sems, halo_sems, store_sems, own_sem, fixed_sem,
+    want_sems, there_sems, back_sems, halo_sems, store_sems, own_sem, fixed_sem, speed_sem, base_sem,
 ):
     z_cells, y_cells, _ = tpl_ref.shape
     me = lax.axis_index("slab")
@@ -234,6 +235,8 @@
     z_head, y_head = pl.ds(0, 1), pl.ds(0, 8)
     fixed = pltpu.make_async_copy(fixed_ref, miss_ref, fixed_sem)
     fixed.start()
+    speed = pltpu.make_async_copy(vel_ref, speed_ref, speed_sem)
+    speed.start()
     meet(count)
 
     def want(j):
@@ -284,6 +287,26 @@
         return carry
 
     lax.fori_loop(0, CHUNKS, there, 0)
+    for halo in halos:
+        halo.wait()
+    speed.wait()
+
+    def smooth(z, carry):
+        for c in range(3):
+            here = speed_ref[c, z]
+            before_z = jnp.where(z == 0, keep_below * vz_low[c, 0], speed_ref[c, jnp.maximum(z - 1, 0)])
+            after_z = jnp.where(
+                z == z_cells - 1, keep_above * vz_high[c, 0], speed_ref[c, jnp.minimum(z + 1, z_cells - 1)]
+            )
+            before_y, after_y = next_y(here, keep_left * vy_low[c, z, 7:8], keep_right * vy_high[c, z, 0:1])
+            before_x, after_x = next_x(here)
+            around = (before_z + after_z) + (before_y + after_y) + (before_x + after_x)
+            total_ref[c, z] = smooth_weight * (6.0 * here - around)
+        return carry
+
+    lax.fori_loop(0, z_cells, smooth, 0)
+    base = pltpu.make_async_copy(total_ref, base_ref, base_sem)
+    base.start()
 
     def back(turn, carry):
         chunk = turn_of(turn)
@@ -309,8 +332,7 @@
         return carry
 
     lax.fori_loop(0, CHUNKS, back, 0)
-    for halo in halos:
-        halo.wait()
+    base.wait()
 
     def plane(z):
         here = tpl_ref[z]
@@ -380,7 +402,7 @@
 
 
 def gradient_kernel(
-    vel_ref, vel_before_ref, vel_after_ref, vz_low_ref, vz_high_ref, vy_low_ref, vy_high_ref,
+    vel_ref, base_ref,
     frc_ref, frc_before_ref, frc_after_ref, fz_low_ref, fz_high_ref, fy_low_ref, fy_high_ref, out_ref,
 ):
     block = pl.program_id(0)
@@ -410,11 +432,9 @@
     for z in range(planes):
         half = [0.5 * time_step * vel_ref[i, z] for i in range(3)]
         for c in range(3):
-            v = around(vel_ref, vel_before_ref, vel_after_ref, vz_low_ref, vz_high_ref, vy_low_ref[c, z, 7:8], vy_high_ref[c, z, 0:1], c, z)
-            laplace = 6.0 * v[0] - (((v[1] + v[2]) + (v[3] + v[4])) + (v[5] + v[6]))
             f = around(frc_ref, frc_before_ref, frc_after_ref, fz_low_ref, fz_high_ref, fy_low_ref[c, z:z + 1], fy_high_ref[c, z:z + 1], c, z)
             advect = half[0] * (f[2] - f[1]) + half[1] * (f[4] - f[3]) + half[2] * (f[6] - f[5])
-            out_ref[c, z] = smooth_weight * laplace + f[0] - advect
+            out_ref[c, z] = base_ref[c, z] + f[0] - advect
 
 
 def per_device(template, fixed_image, velocity, src_owner, src_local, weights):
@@ -440,19 +460,19 @@
     packed = pltpu.VMEM((slab_count, depth, EDGE, LANES), f32)
     z_face, y_face = (1, y_cells, x_cells), (z_cells, 8, x_cells)
     edge = (3, z_cells, x_cells)
-    shapes = [(3,) + template.shape, (3,) + z_face, (3,) + z_face, edge, edge]
-    shapes += [(3,) + z_face, (3,) + z_face, (3,) + y_face, (3,) + y_face]
+    shapes = [(3,) + template.shape, (3,) + template.shape, (3,) + z_face, (3,) + z_face, edge, edge]
     field = pltpu.VMEM(template.shape, f32)
     block_sems = pltpu.SemaphoreType.DMA((2, CHUNKS * slab_count))
-    force, fz_low, fz_high, fy_low, fy_high, vz_low, vz_high, vy_low, vy_high = pl.pallas_call(
+    force, base, fz_low, fz_high, fy_low, fy_high = pl.pallas_call(
         functools.partial(main_kernel, slab_count),
         out_shape=[jax.ShapeDtypeStruct(shape, f32) for shape in shapes],
         in_specs=[whole()] * 4 + [whole(pl.ANY)] * 2,
-        out_specs=[whole(pl.ANY)] * 9,
-        scratch_shapes=[pltpu.VMEM(spread, i32)] + [packed] * 4 + [field] * 2 + [pltpu.VMEM((3,) + template.shape, f32)]
+        out_specs=[whole(pl.ANY)] * 6,
+        scratch_shapes=[pltpu.VMEM(spread, i32)] + [packed] * 4 + [field] * 2 + [pltpu.VMEM((3,) + template.shape, f32)] * 2
+        + [pltpu.VMEM((3,) + z_face, f32)] * 2 + [pltpu.VMEM((3,) + y_face, f32)] * 2
         + [pltpu.VMEM(z_face, f32)] * 2 + [pltpu.VMEM(y_face, f32)] * 2 + [pltpu.VMEM(edge, f32)] * 2
         + [pltpu.SemaphoreType.DMA((2, slab_count)), block_sems, block_sems, pltpu.SemaphoreType.DMA((2, 12))]
-        + [pltpu.SemaphoreType.DMA((CHUNKS * (EDGE // depth),)), pltpu.SemaphoreType.DMA, pltpu.SemaphoreType.DMA],
+        + [pltpu.SemaphoreType.DMA((CHUNKS * (EDGE // depth),)), pltpu.SemaphoreType.DMA] + [pltpu.SemaphoreType.DMA] * 3,
         compiler_params=params(collective_id=1, has_side_effects=True),
         name="transport",
     )(ids, brick_of, slot_weight, template, fixed_image, velocity)
@@ -469,18 +489,17 @@
         z_spec,
         z_spec,
     ]
-    vy_spec = pl.BlockSpec((3, rows, 8, x_cells), lambda z: (0, z, 0, 0))
     fy_spec = pl.BlockSpec((3, rows, x_cells), lambda z: (0, z, 0))
     return pl.pallas_call(
         gradient_kernel,
         grid=(z_cells // rows,),
         out_shape=jax.ShapeDtypeStruct(velocity.shape, f32),
-        in_specs=field_specs + [vy_spec] * 2 + field_specs + [fy_spec] * 2,
+        in_specs=field_specs[:1] * 2 + field_specs + [fy_spec] * 2,
         out_specs=pl.BlockSpec(block, lambda z: (0, z, 0, 0)),
         compiler_params=params(),
         name="gradient",
     )(
-        velocity, velocity, velocity, vz_low, vz_high, vy_low, vy_high,
+        velocity, base,
         force, force, force, fz_low, fz_high, fy_low, fy_high,
     )
 

time: 131 us -> 135 us (1.031)
  Pallas kernels: 131 us -> 135 us
    pallas_call x1, Pallas kernels: 115 us -> 121 us  [per_device(): pl.pallas_call(functools.partial(main_kernel, slab_count), out_shape=[jax...]
    pallas_call x1, Pallas kernels: 13.5 us -> 11.6 us  [per_device(): pl.pallas_call(gradient_kernel, grid=(z_cells // rows,), out_shape=jax.Sh...]
where the time goes in v3:
time: 135 us
  Pallas kernels  135 us (100%)
    pallas_call x1, Pallas kernels, per_device(): pl.pallas_call(functools.partial(main_kernel, slab_count), out_shape=[jax...  121 us
    pallas_call x1, Pallas kernels, per_device(): pl.pallas_call(gradient_kernel, grid=(z_cells // rows,), out_shape=jax.Sh...  11.6 us

profile of v3, /device:TPU:0, one launch (start us, length us, event | category | flops | bytes accessed | tf_op | source)
XLA Modules:
  0.0 134.9 jit_solution(4601706422586954075)
XLA Ops:
  0.0 1.9 %slots.1 = (s32[8,8,128]{2,1,0:T(8,128)}, s32[8,8,128]{2,1,0:T(8,128)}, f32[8,8,128]{2,1,0:T(8,128)}) custom-call(s32[2,16]{1,0:T(2,128)} %bitcast.3, s32[2,16]{1,0:T(2,128)} %bitcast.4, f32[2,16]{1,0:T(2,128)} %bitcast.5), custom_call_target="tpu_custom_call" | custom-call | tf_op jit(solution)/shard_map/slots/pallas_call | solution.py:451
  1.9 121.5 %transport.1 = (f32[3,32,64,256]{3,2,1,0:T(8,128)}, f32[3,32,64,256]{3,2,1,0:T(8,128)}, f32[3,1,64,256]{3,2,1,0:T(8,128)}, f32[3,1,64,256]{3,2,1,0:T(8,128)}, f3...) custom-call(s32[8,8,128]{2,1,0:T(8,128)} %get-tuple-element.14.ids_ref, s32[8,8,128]{2,1,0:T(8,128)} %get-tuple-element.15.brick_ref, ...), custom_call_target="tpu_custom_call" | custom-call | tf_op jit(solution)/shard_map/transport/pallas_call | solution.py:466
  123.3 11.6 %gradient.1 = f32[3,32,64,256]{3,2,1,0:T(8,128)} custom-call(f32[3,32,64,256]{3,2,1,0:T(8,128)} %vel_ref.3, f32[3,32,64,256]{3,2,1,0:T(8,128)} %get-tuple-element.17.base_ref, f32[3,32,64,256]{3,2,1,0:T(8,128)} %get-tuple-element.18.frc_ref.frc_before_ref.frc_after_ref, f32[3,32,64,256]{3,2,1,0:T(8,128)} %get-tuple-element.18.frc_ref.frc_before_ref.frc_after_ref, ...), custom_call_target="tpu_custom_call" | custom-call | tf_op jit(solution)/shard_map/gradient/pallas_call | solution.py:493
